TPU v7x, 128 devices: a whole 4x4x4 slice. The times are simulated.
128 devices in a mesh: cfg: 2 (over z_lo), seq: 8 (over x, core), blk: 8 (over z_hi, y).
Axes of the slice: x: 4, y: 4, z: 4 (z_hi: 2, z_lo: 2; z = z_hi * 2 + z_lo), core: 2. Of those that a mesh axis runs over, the one named last changes fastest.
Arguments:
- hidden: bfloat16 [2, 3072, 5120], P('cfg', 'seq', 'blk'), may hold values from -2.5 to 2.5
- modulation: float32 [3, 5120], replicated, may hold values from -4 to 4
- in_projection: bfloat16 [5120, 3, 3072], P(('cfg', 'seq'), None, 'blk'), may hold values from -0.078125 to 0.078125
- out_projection: bfloat16 [3072, 5120], P('blk', ('cfg', 'seq')), may hold values from -0.15625 to 0.15625
- lengths: int32 [5], replicated, may hold values from 1 to 1536, 3072 in all
- positions: int32 [3, 3072], P(None, 'seq'), may hold values from 0 to 63
- guidance: float32 [1], replicated, may hold values from 2 to 5
Outputs:
- guided: float32 [8, 2, 192, 5120], P('seq', 'cfg', None, 'blk')
Inputs may be any that keep to these rules, and one draw needn't show every extreme that they name: The clip lengths sum to 3072 and the longest is exactly 1536.
All inputs are finite; a program needn't handle non-finite values.
Results may differ from a plain program's by a relative error of at most 0.012.
The roundings to bfloat16 on the way count: a program that leaves them out, or rounds other values in their place, can miss the bound.
Values may be sent and summed in bfloat16 or wider, within the bound.
A program may use at most 128 MiB of HBM per device.

v0:
```python
import jax
import jax.numpy as jnp
import numpy as np
from jax import lax
from jax.sharding import Mesh, PartitionSpec as P

HEAD_DIM = 128
SEQ = ("x", "core")
BLK = ("zhi", "y")
SWAP = [(0, 1), (1, 0)]


def rotary_angles(head_width):
    third = head_width // 6
    first_dim = head_width - 4 * third
    other_dim = 2 * third
    pair_index = np.arange(head_width) // 2
    first_pairs = first_dim // 2
    other_pairs = other_dim // 2
    in_first = pair_index < first_pairs
    in_second = (pair_index >= first_pairs) & (pair_index < first_pairs + other_pairs)
    in_third = pair_index >= first_pairs + other_pairs
    row_first = np.where(in_first, 10000.0 ** (-2.0 * pair_index / first_dim), 0.0)
    row_second = np.where(
        in_second, 10000.0 ** (-2.0 * (pair_index - first_pairs) / other_dim), 0.0
    )
    row_third = np.where(
        in_third, 10000.0 ** (-2.0 * (pair_index - first_pairs - other_pairs) / other_dim), 0.0
    )
    return np.stack([row_first, row_second, row_third]).astype(np.float32)


def turn_matrix(head_width):
    row_index = np.arange(head_width)[:, None]
    col_index = np.arange(head_width)[None, :]
    upper = np.where((col_index == row_index + 1) & (row_index % 2 == 0), 1.0, 0.0)
    lower = np.where((col_index == row_index - 1) & (row_index % 2 == 1), -1.0, 0.0)
    return (upper + lower).astype(np.float32)


def layer_norm(inputs):
    row_mean = jnp.mean(inputs, -1, keepdims=True)
    centered = inputs - row_mean
    variance = jnp.mean(centered * centered, -1, keepdims=True)
    return centered * lax.rsqrt(variance + 1e-06)


def rms_norm(inputs):
    return inputs * lax.rsqrt(jnp.mean(inputs * inputs, -1, keepdims=True) + 1e-06)


def rotate(inputs, cosine, sine, turning):
    turned = jnp.einsum("thd,de->the", inputs, turning, precision=lax.Precision.HIGHEST)
    return inputs * cosine + turned * sine


def clip_of(clip_ends, token_index):
    return jnp.sum((token_index[:, None] >= clip_ends[None, :]).astype(jnp.int32), 1)


def local(hidden, modulation, in_projection, out_projection, lengths, positions, guidance):
    cfg = lax.axis_index("cfg")
    core = lax.axis_index("core")
    seq = lax.axis_index("x") * 2 + core
    states = hidden[0]
    tok_count = states.shape[0]
    half_rows = tok_count // 2
    n_blk = lax.axis_size(BLK)
    inner_width = in_projection.shape[2]
    head_count = inner_width // HEAD_DIM
    sent_rows = lax.dynamic_slice_in_dim(states, (1 - cfg) * half_rows, half_rows, 0)
    other_rows = lax.ppermute(sent_rows, "cfg", SWAP)
    mine_rows = lax.dynamic_slice_in_dim(states, cfg * half_rows, half_rows, 0)
    is_cond = cfg == 0
    cond_rows = jnp.where(is_cond, mine_rows, other_rows).astype(jnp.float32)
    uncond_rows = jnp.where(is_cond, other_rows, mine_rows).astype(jnp.float32)
    scale = guidance[0]
    hidden_part = uncond_rows + scale * (cond_rows - uncond_rows)
    full_states = lax.all_gather(states, BLK, axis=1, tiled=True)
    modulated = (
        layer_norm(full_states.astype(jnp.float32)) * (1.0 + modulation[1]) + modulation[0]
    ).astype(jnp.bfloat16)
    w_mine = lax.all_gather(in_projection, ("cfg", "x"), axis=0, tiled=True)
    w_other = lax.ppermute(w_mine, "core", SWAP)
    rows = in_projection.shape[0]
    n_pairs = w_mine.shape[0] // rows
    mod4 = modulated.reshape(tok_count, n_pairs, 2, rows)
    mod_mine = lax.dynamic_index_in_dim(mod4, core, axis=2, keepdims=False)
    mod_other = lax.dynamic_index_in_dim(mod4, 1 - core, axis=2, keepdims=False)
    mixed = jnp.einsum(
        "tjd,jdqe->tqe",
        mod_mine,
        w_mine.reshape(n_pairs, rows, 3, inner_width),
        preferred_element_type=jnp.float32,
    ) + jnp.einsum(
        "tjd,jdqe->tqe",
        mod_other,
        w_other.reshape(n_pairs, rows, 3, inner_width),
        preferred_element_type=jnp.float32,
    )
    mixed = mixed.reshape(tok_count, 3, head_count, HEAD_DIM)
    angle_table = jnp.asarray(rotary_angles(HEAD_DIM))
    turning = jnp.asarray(turn_matrix(HEAD_DIM))
    angles = jnp.einsum(
        "at,ae->te", positions.astype(jnp.float32), angle_table, precision=lax.Precision.HIGHEST
    )
    cosine = jnp.cos(angles)[:, None, :]
    sine = jnp.sin(angles)[:, None, :]
    queries = rotate(rms_norm(mixed[:, 0]), cosine, sine, turning).astype(jnp.bfloat16)
    key_rows = rotate(rms_norm(mixed[:, 1]), cosine, sine, turning).astype(jnp.bfloat16)
    value_rows = mixed[:, 2].astype(jnp.bfloat16)
    kv = jnp.stack([key_rows, value_rows], axis=1)
    kv_mine = lax.all_gather(kv, "x", axis=0, tiled=True)
    kv_other = lax.ppermute(kv_mine, "core", SWAP)
    kv_all = jnp.concatenate([kv_mine, kv_other], axis=0)
    key_piece = kv_all[:, 0]
    value_piece = kv_all[:, 1]
    row_count = key_piece.shape[0]
    n_x = kv_mine.shape[0] // tok_count
    clip_ends = jnp.cumsum(lengths)
    query_clip = clip_of(clip_ends, seq * tok_count + jnp.arange(tok_count, dtype=jnp.int32))
    key_row = jnp.arange(row_count, dtype=jnp.int32)
    key_block = key_row // tok_count
    key_core = jnp.where(key_block < n_x, core, 1 - core)
    key_token = (key_block % n_x * 2 + key_core) * tok_count + key_row % tok_count
    key_clip_all = clip_of(clip_ends, key_token)
    score_scale = HEAD_DIM ** (-0.5)
    start_state = (
        jnp.zeros((tok_count, head_count, HEAD_DIM), jnp.float32),
        jnp.zeros((head_count, tok_count), jnp.float32),
    )
    key_block_size = 512 if row_count % 512 == 0 else row_count

    def key_step(block_index, running):
        numerator, denominator = running
        key_slab = lax.dynamic_slice_in_dim(
            key_piece, block_index * key_block_size, key_block_size, 0
        )
        value_slab = lax.dynamic_slice_in_dim(
            value_piece, block_index * key_block_size, key_block_size, 0
        )
        key_clip = lax.dynamic_slice_in_dim(
            key_clip_all, block_index * key_block_size, key_block_size, 0
        )
        scores = (
            jnp.einsum("qhd,khd->hqk", queries, key_slab, preferred_element_type=jnp.float32)
            * score_scale
        )
        same_clip = query_clip[:, None] == key_clip[None, :]
        weights = jnp.where(same_clip[None], jnp.exp(scores), 0.0)
        numerator = numerator + jnp.einsum(
            "hqk,khd->qhd",
            weights.astype(jnp.bfloat16),
            value_slab,
            preferred_element_type=jnp.float32,
        )
        denominator = denominator + jnp.sum(weights, -1)
        return (numerator, denominator)

    numerator, denominator = lax.fori_loop(0, row_count // key_block_size, key_step, start_state)
    attended = (
        (numerator / jnp.transpose(denominator)[:, :, None])
        .astype(jnp.bfloat16)
        .reshape(tok_count, inner_width)
    )
    wo_mine = lax.all_gather(out_projection, ("cfg", "x"), axis=1, tiled=True)
    wo_other = lax.ppermute(wo_mine, "core", SWAP)
    cols = out_projection.shape[1]
    wo_mine = wo_mine.reshape(inner_width, n_blk, cols)
    wo_other = wo_other.reshape(inner_width, n_blk, cols)
    first_core = core == 0
    wo_full = jnp.stack(
        [jnp.where(first_core, wo_mine, wo_other), jnp.where(first_core, wo_other, wo_mine)], axis=2
    ).reshape(inner_width, n_blk, 2 * cols)
    weight = jnp.where(is_cond, scale, 1.0 - scale)
    gate = modulation[2].reshape(n_blk, 2 * cols) * weight
    partial = (
        jnp.einsum(
            "rte,ebn->rbtn",
            attended.reshape(2, half_rows, inner_width),
            wo_full,
            preferred_element_type=jnp.float32,
        )
        * gate[None, :, None, :]
    )
    projected = lax.psum_scatter(
        partial.reshape(2 * n_blk, half_rows, 2 * cols),
        ("cfg",) + BLK,
        scatter_dimension=0,
        tiled=True,
    )
    guided = hidden_part + projected[0]
    return guided.reshape(1, 1, half_rows, 2 * cols)


def solution(mesh):
    devices = mesh.devices.reshape(2, 4, 2, 2, 4)
    own = Mesh(devices, ("cfg", "x", "core", "zhi", "y"))
    return jax.shard_map(
        local,
        mesh=own,
        in_specs=(
            P("cfg", SEQ, BLK),
            P(),
            P(("cfg",) + SEQ, None, BLK),
            P(BLK, ("cfg",) + SEQ),
            P(),
            P(None, SEQ),
            P(),
        ),
        out_specs=P(SEQ, "cfg", None, BLK),
        check_vma=False,
    )
```

profile of v0, /device:TPU:0, one launch (start us, length us, event | category | flops | bytes accessed | tf_op | source)
XLA Modules:
  0.0 382.0 jit_solution(14357220380822101249)
XLA Ops:
  7.3 2.0 copy.34
  9.4 70.6 %all-gather.8.cloned.1.call-done = bf16[2560,3,384]{2,0,1:T(8,128)(2,1)} async-done(((bf16[320,3,384]{2,0,1:T(8,128)(2,1)}), bf16[2560,3,384]{2,0,1:T(8,128)(2,1)}) %all-gather.8.cloned.1.call-update) | async-done | bytes 5898256 | tf_op jit(solution)/shard_map/all_gather | solution.py:83
  80.8 1.8 cosine_bitcast_fusion
  84.0 66.6 %all-gather.12.cloned.1.call-done = bf16[1,384,5120]{1,2,0:T(8,128)(2,1)} async-done(((bf16[1,384,640]{1,2,0:T(8,128)(2,1)}), bf16[1,384,5120]{1,2,0:T(8,128)(2,1)}) %all-gather.12.cloned.1.call-update) | async-done | bytes 3932176 | tf_op jit(solution)/shard_map/all_gather | solution.py:79
  150.6 3.0 convert_reduce_fusion
  155.0 2.9 fusion.20
  158.0 3.3 fusion.23
  161.3 6.0 %bitcast_add_fusion = f32[384,3,384]{0,2,1:T(8,128)S(1)} fusion(f32[384,3,384,1]{0,2,3,1:T(8,128)S(1)} %fusion.23, bf16[8,320,3,384]{3,1,0,2:T(8,128)(2,1)} %bitcast.18, bf16[384,8,2,320]{0,3,2,1:T(8,128)(2,1)S(1)} %bitcast.133, s32[]{:T(128)S(6)} %select_n.127), kind=kOutput, calls=%fused_computation.38 | convolution fusion | flops 2265366528 | bytes 11403268 | tf_op jit(solution)/shard_map/tjd,jdqe->tqe/dot_general | solution.py:95
  170.7 20.4 %all-gather.6.cloned.1.call-done = bf16[384,2560]{0,1:T(8,128)(2,1)} async-done(((bf16[384,320]{0,1:T(8,128)(2,1)}), bf16[384,2560]{0,1:T(8,128)(2,1)}) %all-gather.6.cloned.1.call-update) | async-done | bytes 1966096 | tf_op jit(solution)/shard_map/all_gather | solution.py:166
  191.9 33.0 %all-gather.10.cloned.1.call-done = bf16[1536,2,3,128]{3,0,2,1:T(8,128)(2,1)} async-done(((bf16[384,2,3,128]{3,0,2,1:T(8,128)(2,1)}), bf16[1536,2,3,128]{3,0,2,1:T(8,128)(2,1)}) %all-gather.10.cloned.1.call-update) | async-done | bytes 2359312 | tf_op jit(solution)/shard_map/all_gather | solution.py:113
  225.7 1.9 broadcast_select_fusion.1
  227.6 2.3 pad_maximum_fusion
  231.5 2.5 fusion.32
  234.1 2.0 constant_dynamic-update-slice_fusion
  236.1 2.5 slice_bitcast_fusion
  238.6 26.7 %while.16 = (s32[]{:T(128)}, f32[384,3,128]{0,2,1:T(8,128)S(1)}, f32[3,384]{1,0:T(4,128)S(1)}, bf16[3072,3,128]{2,0,1:T(8,128)(2,1)}, s32[384]{0:T(512)S(1)}, /*...) while((s32[]{:T(128)}, f32[384,3,128]{0,2,1:T(8,128)S(1)}, ...), condition=%wide.region_9.10_spmd.clone, body=%wide.region_7.9_spmd.clone.sunk | while | flops 306021504 | bytes 7595706 | solution.py:160
  239.5 1.7 fusion.77
  241.2 1.7 fusion.78
  244.0 1.7 fusion.77
  245.7 1.7 fusion.78
  248.4 1.7 fusion.77
  250.2 1.7 fusion.78
  252.9 1.7 fusion.77
  254.6 1.7 fusion.78
  257.3 1.7 fusion.77
  259.0 1.7 fusion.78
  263.5 1.7 fusion.78
  266.3 4.3 %multiply_bitcast_fusion = f32[2,8,192,640]{3,2,0,1:T(8,128)S(1)} fusion(f32[8,640]{1,0:T(8,128)S(1)} %copy-done.5, bf16[384,8,640,1]{0,2,3,1:T(8,128)(2,1)} %bitcast.129, bf16[2,192,384]{2,1,0:T(8,128)(2,1)S(1)} %copy.50), kind=kOutput, calls=%fused_computation.26 | convolution fusion | flops 1511915520 | bytes 12111872 | tf_op jit(solution)/shard_map/rte,ebn->rbtn/dot_general | solution.py:178
  270.7 3.6 copy.43
  276.9 6.8 %collective-permute-done = bf16[192,640]{1,0:T(8,128)(2,1)S(1)} collective-permute-done((bf16[192,640]{1,0:T(8,128)(2,1)S(1)}, bf16[192,640]{1,0:T(8,128)(2,1)S(1)}, u32[]{:S(2)}, u32[]{:S(2)}) %collective-permute-start) | collective-permute-done | bytes 245792 | tf_op jit(solution)/shard_map/ppermute | solution.py:72
  283.7 89.8 %reduce-scatter.2.cloned.1.call-done = f32[1,192,640]{2,1,0:T(8,128)} async-done(((f32[16,192,640]{2,1,0:T(8,128)}), f32[1,192,640]{2,1,0:T(8,128)}) %reduce-scatter.2.cloned.1.call-update) | async-done | bytes 491536 | tf_op jit(solution)/shard_map/reduce_scatter | solution.py:186
  373.6 1.9 fusion.38
  (89 shorter events, 21.5 us)
Async XLA Ops:
  6.5 73.5 %all-gather.8.cloned.1.call-start = ((), (), s32[]{:S(2)}) async-start(), calls=%async_computation.2 | async-start | bytes 6635520 | tf_op jit(solution)/shard_map/all_gather | solution.py:83
  7.3 143.4 %all-gather.12.cloned.1.call-start = ((), (), s32[]{:S(2)}) async-start(), calls=%async_computation.5 | async-start | bytes 4423680 | tf_op jit(solution)/shard_map/all_gather | solution.py:79
  9.3 181.8 %all-gather.6.cloned.1.call-start = ((), (), s32[]{:S(2)}) async-start(), calls=%async_computation.1 | async-start | bytes 2211840 | tf_op jit(solution)/shard_map/all_gather | solution.py:166
  80.0 81.2 %collective-permute-start.2 = (bf16[2560,3,384]{2,0,1:T(8,128)(2,1)}, bf16[2560,3,384]{2,0,1:T(8,128)(2,1)}, u32[]{:S(2)}, u32[]{:S(2)}) collective-permute-start(bf16[2560,3,384]{2,0,1:T(8,128)(2,1)} %all-gather.8.cloned.1.call-done), channel_id=1, source_target_pairs={{0,8},{8,0},{1,9},{9,1},{2,10},{10,2},{3,11},{11,3},{4,12},{12,4},... | collective-permute-start | bytes 17694728 | tf_op jit(solution)/shard_map/ppermute | solution.py:84
  80.1 144.8 %all-gather.10.cloned.1.call-start = ((), (), s32[]{:S(2)}) async-start(), calls=%async_computation.3 | async-start | bytes 2949120 | tf_op jit(solution)/shard_map/all_gather | solution.py:113
  82.7 86.4 %copy-start.3 = (f32[384,128]{1,0:T(8,128)}, f32[384,128]{1,0:T(8,128)S(1)}, u32[]{:S(2)}) copy-start(f32[384,128]{1,0:T(8,128)S(1)} %copy.36) | copy-start | bytes 589828
  82.8 86.2 %copy-start.4 = (f32[384,128]{1,0:T(8,128)}, f32[384,128]{1,0:T(8,128)S(1)}, u32[]{:S(2)}) copy-start(f32[384,128]{1,0:T(8,128)S(1)} %copy.37) | copy-start | bytes 589828
  150.6 3.3 copy-start
  153.9 4.0 %slice-start = ((s8[5898240]{0:T(1024)(128)(4,1)}), s8[4194304]{0:T(1024)(128)(4,1)S(1)}, s32[]{:S(2)}) async-start(s8[5898240]{0:T(1024)(128)(4,1)} %bitcast.141), calls=%async_computation.6 | async-start | bytes 8388608
  155.0 2.9 slice-start.1
  167.3 1.8 copy-start.7
  167.4 23.8 %copy-start.8 = (s32[5]{0:T(128)S(1)}, s32[5]{0:T(128)}, u32[]{:S(2)}) copy-start(s32[5]{0:T(128)} %param.15) | copy-start | bytes 64
  170.7 202.9 %reduce-scatter.2.cloned.1.call-start = ((), (), s32[]{:S(2)}) async-start(), calls=%async_computation.4 | async-start | bytes 8355840 | tf_op jit(solution)/shard_map/reduce_scatter | solution.py:186
  191.1 34.6 %collective-permute-start.1 = (bf16[384,2560]{0,1:T(8,128)(2,1)}, bf16[384,2560]{0,1:T(8,128)(2,1)S(1)}, u32[]{:S(2)}, u32[]{:S(2)}) collective-permute-start(bf16[384,2560]{0,1:T(8,128)(2,1)} %all-gather.6.cloned.1.call-done), channel_id=1, source_target_pairs={{0,8},{8,0},{1,9},{9,1},{2,10},{10,2},{3,11},{11,3},{4,12},{12,4},... | collective-permute-start | bytes 5898248 | tf_op jit(solution)/shard_map/ppermute | solution.py:167
  224.9 9.2 %collective-permute-start.3 = (bf16[1536,2,3,128]{3,0,2,1:T(8,128)(2,1)}, bf16[1536,2,3,128]{3,0,2,1:T(8,128)(2,1)}, u32[]{:S(2)}, u32[]{:S(2)}) collective-permute-start(bf16[1536,2,3,128]{3,0,2,1:T(8,128)(2,1)} %all-gather.10.cloned.1.call-done), channel_id=1, source_target_pairs={{0,8},{8,0},{1,9},{9,1},{2,10},{10,2},{3,11},{11,3},{4,12},{12,4},... | collective-permute-start | bytes 7077896 | tf_op jit(solution)/shard_map/ppermute | solution.py:114
  227.6 6.3 %copy-start.1 = (bf16[1536,2,3,128]{3,0,2,1:T(8,128)(2,1)S(1)}, bf16[1536,2,3,128]{3,0,2,1:T(8,128)(2,1)}, u32[]{:S(2)}) copy-start(bf16[1536,2,3,128]{3,0,2,1:T(8,128)(2,1)} %all-gather.10.cloned.1.call-done) | copy-start | bytes 7077892
  236.1 2.5 copy-start.6
  238.6 27.7 %copy-start.5 = (f32[8,640]{1,0:T(8,128)S(1)}, f32[8,640]{1,0:T(8,128)}, u32[]{:S(2)}) copy-start(f32[8,640]{1,0:T(8,128)} %mul.177) | copy-start | bytes 61444
  274.2 1.0 copy-start.2
  275.3 8.4 %collective-permute-start = (bf16[192,640]{1,0:T(8,128)(2,1)S(1)}, bf16[192,640]{1,0:T(8,128)(2,1)S(1)}, u32[]{:S(2)}, u32[]{:S(2)}) collective-permute-start(bf16[192,640]{1,0:T(8,128)(2,1)S(1)} %dynamic-slice_bitcast_fusion), channel_id=1, source_target_pairs={{0,64},{64,0},{1,65},{65,1},{2,66},{66,2},{3,67},{67,3},{4,68},{68... | collective-permute-start | bytes 737288 | tf_op jit(solution)/shard_map/ppermute | solution.py:72
Sparse Core Ops, SparseCore 0:
  9.0 71.0 all-gather.7
  82.4 68.2 all-gather.11
  152.3 38.7 all-gather.5
  192.6 32.2 all-gather.9
  274.4 99.1 reduce-scatter.1
where the time goes:
time: 383 us; the launch traced here: 382 us
  waiting for transfers between devices  288 us (75%)
  matrix products  39.3 us (10%)
  local copies, waits for them, and re-layouts  20.7 us (5%)
  other arithmetic  17.8 us (5%)
  between operations  14.1 us (4%)
    reduce_scatter x1, waiting for transfers between devices, local(): lax.psum_scatter(partial.reshape(2 * n_blk, half_rows, 2 * cols), ('cfg',...  89.8 us
    all_gather x1, waiting for transfers between devices, local(): w_mine = lax.all_gather(in_projection, ('cfg', 'x'), axis=0, tiled=True)  70.6 us
    all_gather x1, waiting for transfers between devices, local(): full_states = lax.all_gather(states, BLK, axis=1, tiled=True)  66.6 us
    all_gather x1, waiting for transfers between devices, local(): kv_mine = lax.all_gather(kv, 'x', axis=0, tiled=True)  33 us
    all_gather x1, waiting for transfers between devices, local(): wo_mine = lax.all_gather(out_projection, ('cfg', 'x'), axis=1, tiled=True)  20.4 us
    dot_general x6, matrix products, key_step(): jnp.einsum('qhd,khd->hqk', queries, key_slab, preferred_element_type=jnp....  10.4 us
    dot_general x6, matrix products, key_step(): jnp.einsum('hqk,khd->qhd', weights.astype(jnp.bfloat16), value_slab, pref...  10.4 us
  transfers between devices with their start and end apart: 9, of which 6 were waited for; matrix products, arithmetic and copies ran while one was open for 9% of the time, Pallas kernels for 0%

commit v1 on v0

--- a/solution.py
+++ b/solution.py
@@ -8,6 +8,10 @@
 SEQ = ("x", "core")
 BLK = ("zhi", "y")
 SWAP = [(0, 1), (1, 0)]
+trace_screen_on = lambda in_array, axis_id: jnp.concatenate(
+    lax.all_to_all(jnp.stack([in_array for _ in range(lax.axis_size(axis_id))], 0), axis_id, 0, 0),
+    0,
+)
 
 
 def rotary_angles(head_width):
@@ -80,7 +84,7 @@
     modulated = (
         layer_norm(full_states.astype(jnp.float32)) * (1.0 + modulation[1]) + modulation[0]
     ).astype(jnp.bfloat16)
-    w_mine = lax.all_gather(in_projection, ("cfg", "x"), axis=0, tiled=True)
+    w_mine = trace_screen_on(in_projection, ("cfg", "x"))
     w_other = lax.ppermute(w_mine, "core", SWAP)
     rows = in_projection.shape[0]
     n_pairs = w_mine.shape[0] // rows

time: 383 us -> 370 us (0.966)
  waiting for transfers between devices: 288 us -> 259 us
  local copies, waits for them, and re-layouts: 20.7 us -> 30.1 us
  starting transfers between devices: 1.81 us -> 7.69 us
    all_gather x1 -> x0, waiting for transfers between devices: 70.6 us -> none  [local(): w_mine = lax.all_gather(in_projection, ('cfg', 'x'), axis=0, tiled=True)]
    all_to_all x0 -> x1, waiting for transfers between devices: none -> 66.6 us  [lax.all_to_all(jnp.stack([in_array for _ in range(lax.axis_size(axis_id))...]
    all_gather x1, waiting for transfers between devices: 66.6 us -> 44.6 us  [local(): full_states = lax.all_gather(states, BLK, axis=1, tiled=True)]
    all_to_all x0 -> x1, local copies, waits for them, and re-layouts: none -> 5.9 us  [lax.all_to_all(jnp.stack([in_array for _ in range(lax.axis_size(axis_id))...]
    all_to_all x0 -> x1, starting transfers between devices: none -> 5.9 us  [lax.all_to_all(jnp.stack([in_array for _ in range(lax.axis_size(axis_id))...]
    another operation x0 -> x1, local copies, waits for them, and re-layouts: none -> 4.53 us  [jnp.stack([in_array for _ in range(lax.axis_size(axis_id))], 0)]
  transfers between devices with their start and end apart: 9 -> 9, of which waited for: 6 -> 6; matrix products, arithmetic and copies ran while one was open for 9% -> 11% of each run, Pallas kernels for 0% -> 0%
where the time goes in v1:
time: 370 us; the launch traced here: 369 us
  waiting for transfers between devices  259 us (70%)
  matrix products  41.4 us (11%)
  local copies, waits for them, and re-layouts  30.1 us (8%)
  other arithmetic  16.8 us (5%)
  between operations  14.1 us (4%)
  starting transfers between devices  7.69 us (2%)
    reduce_scatter x1, waiting for transfers between devices, local(): lax.psum_scatter(partial.reshape(2 * n_blk, half_rows, 2 * cols), ('cfg',...  90 us
    all_to_all x1, waiting for transfers between devices, lax.all_to_all(jnp.stack([in_array for _ in range(lax.axis_size(axis_id))...  66.6 us
    all_gather x1, waiting for transfers between devices, local(): full_states = lax.all_gather(states, BLK, axis=1, tiled=True)  44.6 us
    all_gather x1, waiting for transfers between devices, local(): kv_mine = lax.all_gather(kv, 'x', axis=0, tiled=True)  33.1 us
    all_gather x1, waiting for transfers between devices, local(): wo_mine = lax.all_gather(out_projection, ('cfg', 'x'), axis=1, tiled=True)  17.6 us
    dot_general x6, matrix products, key_step(): jnp.einsum('qhd,khd->hqk', queries, key_slab, preferred_element_type=jnp....  10.4 us
    dot_general x6, matrix products, key_step(): jnp.einsum('hqk,khd->qhd', weights.astype(jnp.bfloat16), value_slab, pref...  10.4 us
  transfers between devices with their start and end apart: 9, of which 6 were waited for; matrix products, arithmetic and copies ran while one was open for 11% of the time, Pallas kernels for 0%

profile of v1, /device:TPU:0, one launch (start us, length us, event | category | flops | bytes accessed | tf_op | source)
XLA Modules:
  0.0 369.2 jit_solution(17632639510671701647)
XLA Ops:
  6.5 4.5 %stack.9 = bf16[8,320,3,384]{3,1,2,0:T(8,128)(2,1)} broadcast(bf16[320,3,384]{2,0,1:T(8,128)(2,1)} %param.13), dimensions={1,2,3} | broadcast | bytes 6635520 | tf_op jit(solution)/shard_map/stack | solution.py:12
  11.1 5.9 %all-to-all-start = ((bf16[8,320,3,384]{3,1,2,0:T(8,128)(2,1)}), bf16[8,320,3,384]{3,1,2,0:T(8,128)(2,1)}, u32[]{:S(2)}, u32[]{:S(2)}) async-start(bf16[8,320,3,384]{3,1,2,0:T(8,128)(2,1)} %stack.9), calls=%async_computation | async-start | bytes 11796480 | tf_op jit(solution)/shard_map/all_to_all | solution.py:12
  18.1 66.6 %all-to-all-done = bf16[8,320,3,384]{3,1,2,0:T(8,128)(2,1)} async-done(((bf16[8,320,3,384]{3,1,2,0:T(8,128)(2,1)}), bf16[8,320,3,384]{3,1,2,0:T(8,128)(2,1)}, u32[]{:S(2)}, u32[]{:S(2)}) %all-to-all-start) | async-done | bytes 5898272 | tf_op jit(solution)/shard_map/all_to_all | solution.py:12
  84.7 5.9 %copy.60 = bf16[8,320,3,384]{3,1,0,2:T(8,128)(2,1)} copy(bf16[8,320,3,384]{3,1,2,0:T(8,128)(2,1)} %all-to-all-done) | data formatting | bytes 11796480 | tf_op jit(solution)/shard_map/all_to_all | solution.py:12
  92.9 44.6 %all-gather.9.cloned.1.call-done = bf16[1,384,5120]{1,2,0:T(8,128)(2,1)} async-done(((bf16[1,384,640]{1,2,0:T(8,128)(2,1)}), bf16[1,384,5120]{1,2,0:T(8,128)(2,1)}) %all-gather.9.cloned.1.call-update) | async-done | bytes 3932176 | tf_op jit(solution)/shard_map/all_gather | solution.py:83
  137.4 3.0 convert_reduce_fusion
  141.8 2.9 fusion.20
  144.8 6.0 %fusion.21 = f32[384,3,384,1]{0,2,1,3:T(8,128)S(1)} fusion(bf16[8,320,3,384]{3,1,2,0:T(8,128)(2,1)} %all-to-all-done, bf16[384,8,2,320]{0,3,2,1:T(8,128)(2,1)S(1)} %bitcast.136, s32[]{:T(128)S(6)} %select_n.126), kind=kOutput, calls=%fused_computation.30 | convolution fusion | flops 2264924160 | bytes 9633796 | tf_op jit(solution)/shard_map/tjd,jdqe->tqe/dot_general | solution.py:94
  150.8 6.1 %bitcast_add_fusion = f32[384,3,384]{0,2,1:T(8,128)S(1)} fusion(f32[384,3,384,1]{0,2,1,3:T(8,128)S(1)} %fusion.21, bf16[8,320,3,384]{3,1,0,2:T(8,128)(2,1)} %bitcast.18, bf16[384,8,2,320]{0,3,2,1:T(8,128)(2,1)S(1)} %bitcast.137, s32[]{:T(128)S(6)} %select_n.127), kind=kOutput, calls=%fused_computation.38 | convolution fusion | flops 2265366528 | bytes 11403268 | tf_op jit(solution)/shard_map/tjd,jdqe->tqe/dot_general | solution.py:99
  160.3 17.6 %all-gather.5.cloned.1.call-done = bf16[384,2560]{0,1:T(8,128)(2,1)} async-done(((bf16[384,320]{0,1:T(8,128)(2,1)}), bf16[384,2560]{0,1:T(8,128)(2,1)}) %all-gather.5.cloned.1.call-update) | async-done | bytes 1966096 | tf_op jit(solution)/shard_map/all_gather | solution.py:170
  178.7 33.1 %all-gather.7.cloned.1.call-done = bf16[1536,2,3,128]{3,0,2,1:T(8,128)(2,1)} async-done(((bf16[384,2,3,128]{3,0,2,1:T(8,128)(2,1)}), bf16[1536,2,3,128]{3,0,2,1:T(8,128)(2,1)}) %all-gather.7.cloned.1.call-update) | async-done | bytes 2359312 | tf_op jit(solution)/shard_map/all_gather | solution.py:117
  212.7 1.9 broadcast_select_fusion.1
  214.6 2.3 pad_maximum_fusion
  218.4 2.5 fusion.32
  221.1 2.0 constant_dynamic-update-slice_fusion
  223.0 2.5 slice_bitcast_fusion
  225.5 26.6 %while.16 = (s32[]{:T(128)}, f32[384,3,128]{0,2,1:T(8,128)S(1)}, f32[3,384]{1,0:T(4,128)S(1)}, bf16[3072,3,128]{2,0,1:T(8,128)(2,1)}, s32[384]{0:T(512)S(1)}, /*...) while((s32[]{:T(128)}, f32[384,3,128]{0,2,1:T(8,128)S(1)}, ...), condition=%wide.region_9.10_spmd.clone, body=%wide.region_7.9_spmd.clone.sunk | while | flops 306021504 | bytes 7595706 | solution.py:164
  226.4 1.7 fusion.77
  228.2 1.7 fusion.78
  230.9 1.7 fusion.77
  232.6 1.7 fusion.78
  235.3 1.7 fusion.77
  237.1 1.7 fusion.78
  239.8 1.7 fusion.77
  241.5 1.7 fusion.78
  248.6 1.7 fusion.77
  250.4 1.7 fusion.78
  253.2 4.3 %multiply_bitcast_fusion = f32[2,8,192,640]{3,2,0,1:T(8,128)S(1)} fusion(f32[8,640]{1,0:T(8,128)S(1)} %copy-done.6, bf16[384,8,640,1]{0,2,3,1:T(8,128)(2,1)} %bitcast.133, bf16[2,192,384]{2,1,0:T(8,128)(2,1)S(1)} %copy.77), kind=kOutput, calls=%fused_computation.26 | convolution fusion | flops 1511915520 | bytes 12111872 | tf_op jit(solution)/shard_map/rte,ebn->rbtn/dot_general | solution.py:182
  257.6 3.6 copy.70
  263.9 6.8 %collective-permute-done = bf16[192,640]{1,0:T(8,128)(2,1)S(1)} collective-permute-done((bf16[192,640]{1,0:T(8,128)(2,1)S(1)}, bf16[192,640]{1,0:T(8,128)(2,1)S(1)}, u32[]{:S(2)}, u32[]{:S(2)}) %collective-permute-start) | collective-permute-done | bytes 245792 | tf_op jit(solution)/shard_map/ppermute | solution.py:76
  270.7 90.0 %reduce-scatter.2.cloned.1.call-done = f32[1,192,640]{2,1,0:T(8,128)} async-done(((f32[16,192,640]{2,1,0:T(8,128)}), f32[1,192,640]{2,1,0:T(8,128)}) %reduce-scatter.2.cloned.1.call-update) | async-done | bytes 491536 | tf_op jit(solution)/shard_map/reduce_scatter | solution.py:190
  360.7 1.9 fusion.38
  (93 shorter events, 23.5 us)
Async XLA Ops:
  11.1 5.9 %copy-start.2 = (bf16[1,384,640]{2,1,0:T(8,128)(2,1)S(1)}, bf16[1,384,640]{2,1,0:T(8,128)(2,1)}, u32[]{:S(2)}) copy-start(bf16[1,384,640]{2,1,0:T(8,128)(2,1)} %param.11) | copy-start | bytes 1474564
  11.1 73.7 %all-to-all-start = ((bf16[8,320,3,384]{3,1,2,0:T(8,128)(2,1)}), bf16[8,320,3,384]{3,1,2,0:T(8,128)(2,1)}, u32[]{:S(2)}, u32[]{:S(2)}) async-start(bf16[8,320,3,384]{3,1,2,0:T(8,128)(2,1)} %stack.9), calls=%async_computation | async-start | bytes 11796480 | tf_op jit(solution)/shard_map/all_to_all | solution.py:12
  17.0 120.5 %all-gather.9.cloned.1.call-start = ((), (), s32[]{:S(2)}) async-start(), calls=%async_computation.5 | async-start | bytes 4423680 | tf_op jit(solution)/shard_map/all_gather | solution.py:83
  18.0 73.3 %copy-start.10 = (s32[3,384]{1,0:T(4,128)S(1)}, s32[3,384]{1,0:T(4,128)}, u32[]{:S(2)}) copy-start(s32[3,384]{1,0:T(4,128)} %param.16) | copy-start | bytes 13828
  18.1 73.3 %copy-start.11 = (f32[3,128]{1,0:T(4,128)S(1)}, f32[3,128]{1,0:T(4,128)}, u32[]{:S(2)}) copy-start(f32[3,128]{1,0:T(4,128)} %constant.129.clone) | copy-start | bytes 4612
  18.1 74.7 %copy-start.9 = (f32[3,5120]{1,0:T(4,128)S(1)}, f32[3,5120]{1,0:T(4,128)}, u32[]{:S(2)}) copy-start(f32[3,5120]{1,0:T(4,128)} %param.12) | copy-start | bytes 184324
  18.1 159.8 %all-gather.5.cloned.1.call-start = ((), (), s32[]{:S(2)}) async-start(), calls=%async_computation.2 | async-start | bytes 2211840 | tf_op jit(solution)/shard_map/all_gather | solution.py:170
  90.6 60.1 %collective-permute-start.2 = (bf16[2560,3,384]{2,0,1:T(8,128)(2,1)}, bf16[2560,3,384]{2,0,1:T(8,128)(2,1)}, u32[]{:S(2)}, u32[]{:S(2)}) collective-permute-start(bf16[2560,3,384]{2,0,1:T(8,128)(2,1)} %bitcast.17), channel_id=1, source_target_pairs={{0,8},{8,0},{1,9},{9,1},{2,10},{10,2},{3,11},{11,3},{4,12},{12,4},... | collective-permute-start | bytes 17694728 | tf_op jit(solution)/shard_map/ppermute | solution.py:88
  90.7 121.2 %all-gather.7.cloned.1.call-start = ((), (), s32[]{:S(2)}) async-start(), calls=%async_computation.3 | async-start | bytes 2949120 | tf_op jit(solution)/shard_map/all_gather | solution.py:117
  92.6 66.0 %copy-start.4 = (f32[384,128]{1,0:T(8,128)}, f32[384,128]{1,0:T(8,128)S(1)}, u32[]{:S(2)}) copy-start(f32[384,128]{1,0:T(8,128)S(1)} %copy.63) | copy-start | bytes 589828
  92.7 65.9 %copy-start.5 = (f32[384,128]{1,0:T(8,128)}, f32[384,128]{1,0:T(8,128)S(1)}, u32[]{:S(2)}) copy-start(f32[384,128]{1,0:T(8,128)S(1)} %copy.64) | copy-start | bytes 589828
  137.4 3.3 copy-start
  156.9 1.8 copy-start.8
  156.9 21.0 %copy-start.12 = (s32[5]{0:T(128)S(1)}, s32[5]{0:T(128)}, u32[]{:S(2)}) copy-start(s32[5]{0:T(128)} %param.15) | copy-start | bytes 64
  160.2 200.4 %reduce-scatter.2.cloned.1.call-start = ((), (), s32[]{:S(2)}) async-start(), calls=%async_computation.4 | async-start | bytes 8355840 | tf_op jit(solution)/shard_map/reduce_scatter | solution.py:190
  177.9 34.7 %collective-permute-start.1 = (bf16[384,2560]{0,1:T(8,128)(2,1)}, bf16[384,2560]{0,1:T(8,128)(2,1)S(1)}, u32[]{:S(2)}, u32[]{:S(2)}) collective-permute-start(bf16[384,2560]{0,1:T(8,128)(2,1)} %all-gather.5.cloned.1.call-done), channel_id=1, source_target_pairs={{0,8},{8,0},{1,9},{9,1},{2,10},{10,2},{3,11},{11,3},{4,12},{12,4},... | collective-permute-start | bytes 5898248 | tf_op jit(solution)/shard_map/ppermute | solution.py:171
  211.9 9.2 %collective-permute-start.3 = (bf16[1536,2,3,128]{3,0,2,1:T(8,128)(2,1)}, bf16[1536,2,3,128]{3,0,2,1:T(8,128)(2,1)}, u32[]{:S(2)}, u32[]{:S(2)}) collective-permute-start(bf16[1536,2,3,128]{3,0,2,1:T(8,128)(2,1)} %all-gather.7.cloned.1.call-done), channel_id=1, source_target_pairs={{0,8},{8,0},{1,9},{9,1},{2,10},{10,2},{3,11},{11,3},{4,12},{12,4},... | collective-permute-start | bytes 7077896 | tf_op jit(solution)/shard_map/ppermute | solution.py:118
  214.6 6.3 %copy-start.1 = (bf16[1536,2,3,128]{3,0,2,1:T(8,128)(2,1)S(1)}, bf16[1536,2,3,128]{3,0,2,1:T(8,128)(2,1)}, u32[]{:S(2)}) copy-start(bf16[1536,2,3,128]{3,0,2,1:T(8,128)(2,1)} %all-gather.7.cloned.1.call-done) | copy-start | bytes 7077892
  223.0 2.5 copy-start.7
  225.5 27.7 %copy-start.6 = (f32[8,640]{1,0:T(8,128)S(1)}, f32[8,640]{1,0:T(8,128)}, u32[]{:S(2)}) copy-start(f32[8,640]{1,0:T(8,128)} %mul.177) | copy-start | bytes 61444
  261.2 1.0 copy-start.3
  262.2 8.5 %collective-permute-start = (bf16[192,640]{1,0:T(8,128)(2,1)S(1)}, bf16[192,640]{1,0:T(8,128)(2,1)S(1)}, u32[]{:S(2)}, u32[]{:S(2)}) collective-permute-start(bf16[192,640]{1,0:T(8,128)(2,1)S(1)} %dynamic-slice_bitcast_fusion), channel_id=1, source_target_pairs={{0,64},{64,0},{1,65},{65,1},{2,66},{66,2},{3,67},{67,3},{4,68},{68... | collective-permute-start | bytes 737288 | tf_op jit(solution)/shard_map/ppermute | solution.py:76
Sparse Core Ops, SparseCore 0:
  20.1 117.2 all-gather.8
  139.1 38.7 all-gather.4
  179.6 32.2 all-gather.6
  261.3 99.3 reduce-scatter.1
